TPU v7x, 256 devices: a whole 4x4x8 slice. The times are simulated.
256 devices in a mesh: frame: 16 (over x, z_lo), fsdp: 16 (over z_hi, y, core).
Axes of the slice: x: 4, y: 4, z: 8 (z_hi: 2, z_lo: 4; z = z_hi * 4 + z_lo), core: 2. Of those that a mesh axis runs over, the one named last changes fastest.
Arguments:
- queries: bfloat16 [256, 192, 3072], P(('frame', 'fsdp')), may hold values from -18 to 18
- keys: bfloat16 [256, 192, 3072], P(('frame', 'fsdp')), may hold values from -7 to 7
- values: bfloat16 [256, 192, 3072], P(('frame', 'fsdp')), may hold values from -6 to 6
- residual: bfloat16 [256, 192, 3072], P(('frame', 'fsdp')), may hold values from -6 to 6
- target: bfloat16 [256, 192, 3072], P(('frame', 'fsdp')), may hold values from -6 to 6
- output_weight: bfloat16 [3072, 3072], P('fsdp'), may hold values from -0.109375 to 0.109375
- down_adapter: bfloat16 [16, 64, 3072], P('frame', None, 'fsdp'), may hold values from -0.109375 to 0.109375
- up_adapter: bfloat16 [16, 64, 3072], P('frame', None, 'fsdp'), may hold values from -1.1953125 to 1.1953125
- scene_of_frame: int32 [256], P(('frame', 'fsdp')), may hold values from 0 to 15
- scene_adapter_row: int32 [16], replicated, may hold values from 0 to 15, each once
- valid_token_count: int32 [256], P(('frame', 'fsdp')), may hold values from 1 to 192, 30720 in all
Outputs:
- grad_down: float32 [16, 64, 3072], P('frame', None, 'fsdp')
- grad_up: float32 [16, 64, 3072], P('frame', None, 'fsdp')
- frame_loss: float32 [256], P(('frame', 'fsdp'))
Inputs may be any that keep to these rules, and one draw needn't show every extreme that they name: `scene_adapter_row`: each scene has its own adapter row. `valid_token_count`: some frame has all 192 slots valid.
All inputs are finite; a program needn't handle non-finite values. No bound on the sum of `valid_token_count` on one device may be relied on, other than what follows from the above.
Results may differ from a plain program's by a relative error of at most 0.0053.
Values may be sent and summed in bfloat16 or wider, within the bound.
A program may use at most 192 MiB of HBM per device.

v0:
```python
import math
import jax
import jax.numpy as jnp
from jax import lax
from jax.sharding import PartitionSpec as P

HEADS = 24
adapter_scale = 2.0


def slot_lookup(scene_ids, scene_adapter_row):
    scene_range = jnp.arange(scene_adapter_row.shape[0], dtype=jnp.int32)
    matches = scene_ids[:, None] == scene_range[None, :]
    return jnp.sum(jnp.where(matches, scene_adapter_row[None, :], 0), axis=1)


def per_device(
    queries,
    keys,
    values,
    residual,
    target,
    output_weight,
    down_adapter,
    up_adapter,
    scene_of_frame,
    scene_adapter_row,
    valid_token_count,
):
    frames, slot_count, model_width = queries.shape
    head_count = HEADS
    head_size = model_width // head_count
    row_count = frames * slot_count
    score_scale = 1.0 / math.sqrt(head_size)
    query_heads = queries.reshape(frames, slot_count, head_count, head_size)
    key_heads = keys.reshape(frames, slot_count, head_count, head_size)
    value_heads = values.reshape(frames, slot_count, head_count, head_size)
    scores = (
        jnp.einsum("fqhd,fkhd->fhqk", query_heads, key_heads, preferred_element_type=jnp.float32)
        * score_scale
    )
    positions = lax.broadcasted_iota(jnp.int32, (frames, slot_count), 1)
    valid_mask = positions < valid_token_count[:, None]
    scores = jnp.where(valid_mask[:, None, None, :], scores, -jnp.inf)
    row_max = jnp.max(scores, axis=-1, keepdims=True)
    exponent = jnp.exp(scores - row_max)
    weights = (exponent / jnp.sum(exponent, axis=-1, keepdims=True)).astype(jnp.bfloat16)
    attended = jnp.einsum(
        "fhqk,fkhd->fqhd", weights, value_heads, preferred_element_type=jnp.float32
    )
    attended = attended.astype(jnp.bfloat16).reshape(frames, slot_count, model_width)
    mixed_flat = attended.reshape(row_count, model_width)
    projected_tokens = jnp.dot(
        mixed_flat,
        lax.all_gather(output_weight, "fsdp", axis=0, tiled=True),
        preferred_element_type=jnp.float32,
    )
    projected_tokens = projected_tokens.reshape(frames, slot_count, model_width)
    column_ids = lax.all_gather(scene_of_frame, "fsdp", axis=0, tiled=True)
    column_slots = slot_lookup(column_ids, scene_adapter_row)
    owner_range = jnp.arange(scene_adapter_row.shape[0], dtype=jnp.int32)
    column_pick = column_slots[:, None] == owner_range[None, :]
    adapter_couple = jnp.stack([down_adapter, up_adapter], axis=1)
    blocks = lax.all_gather(adapter_couple, "frame", axis=0, tiled=True)
    chosen = jnp.einsum(
        "fs,sxrd->fxrd",
        column_pick.astype(jnp.bfloat16),
        blocks,
        preferred_element_type=jnp.float32,
    )
    adapters = lax.all_to_all(
        chosen.astype(jnp.bfloat16), "fsdp", split_axis=0, concat_axis=3, tiled=True
    )
    down_weight_rows = adapters[:, 0]
    up_weight_rows = adapters[:, 1]
    low_rank_state = jnp.einsum(
        "ftd,frd->ftr", attended, down_weight_rows, preferred_element_type=jnp.float32
    ).astype(jnp.bfloat16)
    adapter_output = jnp.einsum(
        "akw,awe->ake", low_rank_state, up_weight_rows, preferred_element_type=jnp.float32
    )
    combined_output = (
        residual.astype(jnp.float32)
        + projected_tokens
        + adapter_scale * adapter_output
        - target.astype(jnp.float32)
    )
    residual_error = jnp.where(
        valid_mask[:, :, None], combined_output, jnp.zeros_like(combined_output)
    )
    token_float = valid_token_count.astype(jnp.float32)
    frame_loss = jnp.sum(residual_error * residual_error, axis=(1, 2)) / (token_float * model_width)
    output_gradient = (2.0 * residual_error / token_float[:, None, None]).astype(jnp.bfloat16)
    up_gradient_terms = adapter_scale * jnp.einsum(
        "ftr,ftd->frd", low_rank_state, output_gradient, preferred_element_type=jnp.float32
    )
    backward_low_rank = (
        adapter_scale
        * jnp.einsum(
            "ftd,frd->ftr", output_gradient, up_weight_rows, preferred_element_type=jnp.float32
        )
    ).astype(jnp.bfloat16)
    down_terms = jnp.einsum(
        "ftr,ftd->frd", backward_low_rank, attended, preferred_element_type=jnp.float32
    )
    grad_terms = jnp.stack([down_terms, up_gradient_terms], axis=1)
    pieces = lax.all_to_all(grad_terms, "fsdp", split_axis=3, concat_axis=0, tiled=True)
    scene_dense = jnp.einsum(
        "fs,fxrd->sxrd", column_pick.astype(jnp.float32), pieces, precision=lax.Precision.HIGHEST
    )
    scene_full = lax.psum(scene_dense, "frame")
    owned_rows = lax.dynamic_slice_in_dim(scene_full, lax.axis_index("frame"), 1, 0)
    return (owned_rows[:, 0], owned_rows[:, 1], frame_loss)


def solution(mesh):
    placed = (
        P(("frame", "fsdp"), None, None),
        P(("frame", "fsdp"), None, None),
        P(("frame", "fsdp"), None, None),
        P(("frame", "fsdp"), None, None),
        P(("frame", "fsdp"), None, None),
        P("fsdp", None),
        P("frame", None, "fsdp"),
        P("frame", None, "fsdp"),
        P(("frame", "fsdp")),
        P(),
        P(("frame", "fsdp")),
    )
    return jax.shard_map(
        per_device,
        mesh=mesh,
        in_specs=placed,
        out_specs=(P("frame", None, "fsdp"), P("frame", None, "fsdp"), P(("frame", "fsdp"))),
        check_vma=False,
    )
```

profile of v0, /device:TPU:16, one launch (start us, length us, event | category | flops | bytes accessed | tf_op | source)
XLA Modules:
  0.0 509.0 jit_solution(2743683499181057483)
XLA Ops:
  7.2 0.0 all-gather.2.cloned.1.call-start
  7.2 0.7 all-gather.2.cloned.1.call-update
  8.6 1.3 dynamic-slice
  9.8 0.8 dynamic-update-slice
  10.6 15.7 %all-reduce = s32[16]{0:T(128)S(1)} all-reduce(s32[16]{0:T(128)S(1)} %dynamic-update-slice), channel_id=1, replica_groups=mesh['frame'=16,'fsdp'=16] {'fsdp'}, use_global_device_ids=true, to_apply=%add | all-reduce | flops 16 | bytes 128
  26.3 0.8 select_reduce_fusion
  27.1 0.8 pad_maximum_fusion.1
  27.9 76.0 %all_gather.11 = bf16[16,2,64,192]{3,2,1,0:T(8,128)(2,1)S(1)} all-gather(bf16[1,2,64,192]{3,2,1,0:T(8,128)(2,1)S(1)} %pad_maximum_fusion.1), channel_id=1, replica_groups=mesh['frame'=16,'fsdp'=16] {'frame'}, dimensions={0}, use_global_device_ids=true | all-gather | bytes 835584 | tf_op jit(solution)/shard_map/all_gather | solution.py:64
  103.9 0.7 convolution_convert_fusion
  104.6 0.0 copy-start
  104.6 1.3 copy.63
  106.0 4.8 all-to-all-start
  110.8 0.0 all-reduce.3.cloned.1.call-start
  111.5 0.0 copy-done
  111.5 0.0 copy-start.1
  111.5 0.2 copy.74
  111.7 1.6 copy.75
  113.3 0.0 copy-done.1
  113.3 0.2 copy.76
  113.6 0.8 fusion.24
  114.4 2.0 fusion.51
  116.3 1.1 fusion.15
  117.5 1.8 copy.60
  119.3 54.0 %all-to-all-done = bf16[16,2,64,192]{3,2,1,0:T(8,128)(2,1)S(1)} async-done(((bf16[16,2,64,192]{3,2,1,0:T(8,128)(2,1)}), bf16[16,2,64,192]{3,2,1,0:T(8,128)(2,1)S(1)}, u32[]{:S(2)}, u32[]{:S(2)}) %all-to-all-start) | async-done | bytes 786464 | tf_op jit(solution)/shard_map/all_to_all | solution.py:71
  173.3 0.6 copy.64
  173.9 0.0 copy-start.2
  173.9 1.1 all_to_all.29
  175.0 1.8 fusion.33
  176.8 58.8 %all-gather.2.cloned.1.call-done = bf16[3072,3072]{1,0:T(8,128)(2,1)} async-done(((bf16[192,3072]{1,0:T(8,128)(2,1)}), bf16[3072,3072]{1,0:T(8,128)(2,1)}) %all-gather.2.cloned.1.call-update) | async-done | bytes 18874384 | tf_op jit(solution)/shard_map/all_gather | solution.py:55
  235.6 0.0 copy-done.2
  235.6 0.0 copy-start.3
  235.6 9.1 %fusion.5 = f32[1,192,3072]{2,1,0:T(8,128)S(1)} fusion(bf16[3072,3072]{1,0:T(8,128)(2,1)} %all-gather.2.cloned.1.call-done, bf16[1,192,3072]{2,1,0:T(8,128)(2,1)} %param.14, bf16[24,8,24,128]{3,2,1,0:T(8,128)(2,1)S(1)} %bitcast.107), kind=kOutput, calls=%fused_computation.10 | convolution fusion | flops 3625058304 | bytes 23592960 | tf_op jit(solution)/shard_map/dot_general | solution.py:53
  244.7 0.0 copy-done.3
  244.7 1.5 multiply_reduce_fusion
  246.2 1.3 fusion.7
  247.4 3.2 convolution_bitcast_fusion.1
  250.6 2.7 pad_maximum_fusion
  253.3 4.4 copy.65
  257.8 4.2 reshape.120
  262.0 42.7 %all_to_all.36 = f32[16,1,24576]{2,1,0:T(1,128)S(1)} all-to-all(f32[16,1,24576]{2,1,0:T(1,128)} %reshape.120), channel_id=1, replica_groups=mesh['frame'=16,'fsdp'=16] {'fsdp'}, dimensions={0} | all-to-all | bytes 3145728 | tf_op jit(solution)/shard_map/all_to_all | solution.py:107
  304.7 0.5 broadcast.46
  305.2 6.0 %reduce.5 = f32[16,24576]{1,0:T(8,128)} reduce(f32[16,1,24576]{2,1,0:T(1,128)S(1)} %all_to_all.36, f32[]{:T(128)} %broadcast.46), dimensions={1}, to_apply=%all_to_all.30.reduce_sub_computation | reduce | bytes 3145732 | tf_op jit(solution)/shard_map/all_to_all | solution.py:107
  311.2 3.4 reshape.121
  314.7 3.8 copy.73
  318.5 4.0 fusion.12
  322.5 0.0 all-reduce.3.cloned.1.call-update
  323.2 175.3 %all-reduce.3.cloned.1.call-done = f32[16,2,64,192]{3,0,2,1:T(8,128)} async-done(((f32[16,2,64,192]{3,0,2,1:T(8,128)}), f32[16,2,64,192]{3,0,2,1:T(8,128)}) %all-reduce.3.cloned.1.call-update) | async-done | bytes 1572880 | tf_op jit(solution)/shard_map/psum | solution.py:111
  498.5 1.3 dynamic-slice_bitcast_fusion
  499.8 0.6 copy.67
  500.4 0.6 copy.68
  (2 shorter events, 0.0 us)
Async XLA Ops:
  7.2 228.4 %all-gather.2.cloned.1.call-start = ((), (), s32[]{:S(2)}) async-start(), calls=%async_computation.2 | async-start | bytes 20054016 | tf_op jit(solution)/shard_map/all_gather | solution.py:55
  104.6 6.9 %copy-start = (bf16[1,192,3072]{2,1,0:T(8,128)(2,1)S(1)}, bf16[1,192,3072]{2,1,0:T(8,128)(2,1)}, u32[]{:S(2)}) copy-start(bf16[1,192,3072]{2,1,0:T(8,128)(2,1)} %param.11) | copy-start | bytes 3538948
  106.0 67.3 %all-to-all-start = ((bf16[16,2,64,192]{3,2,1,0:T(8,128)(2,1)}), bf16[16,2,64,192]{3,2,1,0:T(8,128)(2,1)S(1)}, u32[]{:S(2)}, u32[]{:S(2)}) async-start(bf16[16,2,64,192]{3,2,1,0:T(8,128)(2,1)} %copy.63), calls=%async_computation | async-start | bytes 2097152 | tf_op jit(solution)/shard_map/all_to_all | solution.py:71
  110.8 387.7 %all-reduce.3.cloned.1.call-start = ((), (), s32[]{:S(2)}) async-start(), calls=%async_computation.3 | async-start | bytes 4194304 | tf_op jit(solution)/shard_map/psum | solution.py:111
  111.5 1.8 copy-start.1
  173.9 61.7 %copy-start.2 = (bf16[1,192,24,128]{3,2,1,0:T(8,128)(2,1)S(1)}, bf16[1,192,24,128]{3,2,1,0:T(8,128)(2,1)}, u32[]{:S(2)}) copy-start(bf16[1,192,24,128]{3,2,1,0:T(8,128)(2,1)} %copy.60) | copy-start | bytes 3538948
  235.6 9.1 %copy-start.3 = (bf16[1,192,3072]{2,1,0:T(8,128)(2,1)S(1)}, bf16[1,192,3072]{2,1,0:T(8,128)(2,1)}, u32[]{:S(2)}) copy-start(bf16[1,192,3072]{2,1,0:T(8,128)(2,1)} %param.15) | copy-start | bytes 3538948
Sparse Core Ops, SparseCore 0:
  10.7 224.8 all-gather.1
  322.6 175.7 all-reduce.2
where the time goes:
time: 510 us; the launch traced here: 509 us
  waiting for transfers between devices  289 us (57%)
  blocking collectives  134 us (26%)
  local copies, waits for them, and re-layouts  27.8 us (5%)
  matrix products  23.4 us (5%)
  between operations  17.3 us (3%)
  other arithmetic  12.3 us (2%)
    psum x1, waiting for transfers between devices, per_device(): scene_full = lax.psum(scene_dense, 'frame')  175 us
    all_gather x1, blocking collectives, per_device(): blocks = lax.all_gather(adapter_couple, 'frame', axis=0, tiled=True)  76 us
    all_gather x1, waiting for transfers between devices, per_device(): lax.all_gather(output_weight, 'fsdp', axis=0, tiled=True)  58.8 us
    all_to_all x1, waiting for transfers between devices, per_device(): lax.all_to_all(chosen.astype(jnp.bfloat16), 'fsdp', split_axis=0, concat_...  54 us
    all_to_all x1, blocking collectives, per_device(): lax.all_to_all(grad_terms, 'fsdp', split_axis=3, concat_axis=0, tiled=True)  42.7 us
    unnamed x1, blocking collectives  15.7 us
    unnamed x18, local copies, waits for them, and re-layouts  13 us
  transfers between devices with their start and end apart: 3, of which 3 were waited for; matrix products, arithmetic and copies ran while one was open for 3% of the time, Pallas kernels for 0%

commit v1 on v0

--- a/solution.py
+++ b/solution.py
@@ -61,7 +61,9 @@
     owner_range = jnp.arange(scene_adapter_row.shape[0], dtype=jnp.int32)
     column_pick = column_slots[:, None] == owner_range[None, :]
     adapter_couple = jnp.stack([down_adapter, up_adapter], axis=1)
-    blocks = lax.all_gather(adapter_couple, "frame", axis=0, tiled=True)
+    blocks = jnp.concatenate(
+        lax.all_to_all(jnp.stack([adapter_couple] * lax.axis_size("frame")), "frame", 0, 0), axis=0
+    )
     chosen = jnp.einsum(
         "fs,sxrd->fxrd",
         column_pick.astype(jnp.bfloat16),

time: 510 us -> 505 us (level)
  blocking collectives: 134 us -> 72.4 us
  waiting for transfers between devices: 289 us -> 335 us
  starting transfers between devices: 4.89 us -> 17.3 us
    all_gather x1 -> x0, blocking collectives: 76 us -> none  [per_device(): blocks = lax.all_gather(adapter_couple, 'frame', axis=0, tiled=True)]
    all_to_all x1, waiting for transfers between devices: 54 us -> 80.8 us  [per_device(): lax.all_to_all(chosen.astype(jnp.bfloat16), 'fsdp', split_axis=0, concat_...]
    all_to_all x0 -> x1, waiting for transfers between devices: none -> 20.4 us  [per_device(): lax.all_to_all(jnp.stack([adapter_couple] * lax.axis_size('frame')), 'fra...]
    unnamed x1, blocking collectives: 15.7 us -> 27.2 us
    all_to_all x0 -> x1, starting transfers between devices: none -> 8.47 us  [per_device(): lax.all_to_all(jnp.stack([adapter_couple] * lax.axis_size('frame')), 'fra...]
    unnamed x18 -> x26, local copies, waits for them, and re-layouts: 13 us -> 12.9 us
  transfers between devices with their start and end apart: 3 -> 4, of which waited for: 3 -> 4; matrix products, arithmetic and copies ran while one was open for 3% -> 3% of each run, Pallas kernels for 0% -> 0%
where the time goes in v1:
time: 505 us; the launch traced here: 504 us
  waiting for transfers between devices  335 us (66%)
  blocking collectives  72.4 us (14%)
  local copies, waits for them, and re-layouts  27.8 us (6%)
  matrix products  22.2 us (4%)
  between operations  17.4 us (3%)
  starting transfers between devices  17.3 us (3%)
  other arithmetic  11.7 us (2%)
    psum x1, waiting for transfers between devices, per_device(): scene_full = lax.psum(scene_dense, 'frame')  175 us
    all_to_all x1, waiting for transfers between devices, per_device(): lax.all_to_all(chosen.astype(jnp.bfloat16), 'fsdp', split_axis=0, concat_...  80.8 us
    all_gather x1, waiting for transfers between devices, per_device(): lax.all_gather(output_weight, 'fsdp', axis=0, tiled=True)  58.5 us
    all_to_all x1, blocking collectives, per_device(): lax.all_to_all(grad_terms, 'fsdp', split_axis=3, concat_axis=0, tiled=True)  45.2 us
    unnamed x1, blocking collectives  27.2 us
    all_to_all x1, waiting for transfers between devices, per_device(): lax.all_to_all(jnp.stack([adapter_couple] * lax.axis_size('frame')), 'fra...  20.4 us
    unnamed x26, local copies, waits for them, and re-layouts  12.9 us
  transfers between devices with their start and end apart: 4, of which 4 were waited for; matrix products, arithmetic and copies ran while one was open for 3% of the time, Pallas kernels for 0%

profile of v1, /device:TPU:16, one launch (start us, length us, event | category | flops | bytes accessed | tf_op | source)
XLA Modules:
  0.0 504.1 jit_solution(8600168553382813680)
XLA Ops:
  7.2 0.0 copy-start
  7.2 0.0 all-gather.2.cloned.1.call-start
  7.2 0.7 all-gather.2.cloned.1.call-update
  7.9 0.8 maximum_bitcast_fusion
  8.7 1.1 stack.20
  9.8 8.5 %all-to-all-start = ((bf16[16,1,2,64,192]{4,3,2,1,0:T(8,128)(2,1)}), bf16[16,1,2,64,192]{4,3,2,1,0:T(8,128)(2,1)S(1)}, u32[]{:S(2)}, u32[]{:S(2)}) async-start(bf16[16,1,2,64,192]{4,3,2,1,0:T(8,128)(2,1)} %stack.20), calls=%async_computation | async-start | bytes 2097152 | tf_op jit(solution)/shard_map/all_to_all | solution.py:65
  18.3 0.0 copy-start.1
  19.0 0.0 copy-done
  19.0 0.0 copy-start.2
  19.1 0.2 copy.72
  19.3 0.3 copy-done.1
  19.6 0.0 copy-start.7
  19.6 0.0 copy-start.6
  19.6 0.2 copy.73
  19.8 0.6 copy-done.2
  20.4 1.3 copy.74
  22.3 0.0 copy-done.7
  22.4 0.6 dynamic-slice
  22.9 0.8 dynamic-update-slice
  23.7 27.2 %all-reduce = s32[16]{0:T(128)S(1)} all-reduce(s32[16]{0:T(128)S(1)} %dynamic-update-slice), channel_id=1, replica_groups=mesh['frame'=16,'fsdp'=16] {'fsdp'}, use_global_device_ids=true, to_apply=%add | all-reduce | flops 16 | bytes 128
  50.9 0.0 copy-done.6
  50.9 0.2 select_reduce_fusion
  51.1 20.4 %all-to-all-done = bf16[16,1,2,64,192]{4,3,2,1,0:T(8,128)(2,1)S(1)} async-done(((bf16[16,1,2,64,192]{4,3,2,1,0:T(8,128)(2,1)}), bf16[16,1,2,64,192]{4,3,2,1,0:T(8,128)(2,1)S(1)}, u32[]{:S(2)}, u32[]{:S(2)}) %all-to-all-start) | async-done | bytes 786464 | tf_op jit(solution)/shard_map/all_to_all | solution.py:65
  71.5 0.7 convolution_convert_fusion
  72.2 1.3 copy.61
  73.6 8.8 %all-to-all-start.1 = ((bf16[16,2,64,192]{3,2,1,0:T(8,128)(2,1)}), bf16[16,2,64,192]{3,2,1,0:T(8,128)(2,1)S(1)}, u32[]{:S(2)}, u32[]{:S(2)}) async-start(bf16[16,2,64,192]{3,2,1,0:T(8,128)(2,1)} %copy.61), calls=%async_computation.1 | async-start | bytes 2097152 | tf_op jit(solution)/shard_map/all_to_all | solution.py:73
  82.3 0.0 all-reduce.3.cloned.1.call-start
  82.4 0.8 fusion.24
  83.2 0.0 copy-start.3
  83.2 2.0 fusion.52
  85.2 0.0 copy-done.3
  85.2 1.1 fusion.15
  86.3 0.8 copy.58
  87.1 0.0 copy-start.4
  87.1 80.8 %all-to-all-done.1 = bf16[16,2,64,192]{3,2,1,0:T(8,128)(2,1)S(1)} async-done(((bf16[16,2,64,192]{3,2,1,0:T(8,128)(2,1)}), bf16[16,2,64,192]{3,2,1,0:T(8,128)(2,1)S(1)}, u32[]{:S(2)}, u32[]{:S(2)}) %all-to-all-start.1) | async-done | bytes 786464 | tf_op jit(solution)/shard_map/all_to_all | solution.py:73
  167.8 0.6 copy.62
  168.4 1.1 all_to_all.33
  169.6 0.5 fusion.33
  170.1 58.5 %all-gather.2.cloned.1.call-done = bf16[3072,3072]{1,0:T(8,128)(2,1)} async-done(((bf16[192,3072]{1,0:T(8,128)(2,1)}), bf16[3072,3072]{1,0:T(8,128)(2,1)}) %all-gather.2.cloned.1.call-update) | async-done | bytes 18874384 | tf_op jit(solution)/shard_map/all_gather | solution.py:55
  228.6 0.0 copy-done.4
  228.6 0.0 copy-start.5
  228.6 9.1 %fusion.5 = f32[1,192,3072]{2,1,0:T(8,128)S(1)} fusion(bf16[3072,3072]{1,0:T(8,128)(2,1)} %all-gather.2.cloned.1.call-done, bf16[1,192,3072]{2,1,0:T(8,128)(2,1)} %param.14, bf16[24,8,24,128]{3,2,1,0:T(8,128)(2,1)S(1)} %bitcast.112), kind=kOutput, calls=%fused_computation.10 | convolution fusion | flops 3625058304 | bytes 23592960 | tf_op jit(solution)/shard_map/dot_general | solution.py:53
  237.7 0.0 copy-done.5
  237.7 1.5 multiply_reduce_fusion
  239.1 1.3 fusion.7
  240.4 3.2 convolution_bitcast_fusion.1
  243.6 2.7 pad_maximum_fusion
  246.3 4.4 copy.63
  250.7 4.2 reshape.127
  255.0 45.2 %all_to_all.41 = f32[16,1,24576]{2,1,0:T(1,128)S(1)} all-to-all(f32[16,1,24576]{2,1,0:T(1,128)} %reshape.127), channel_id=1, replica_groups=mesh['frame'=16,'fsdp'=16] {'fsdp'}, dimensions={0} | all-to-all | bytes 3145728 | tf_op jit(solution)/shard_map/all_to_all | solution.py:109
  300.1 0.5 broadcast.49
  300.7 6.0 %reduce.5 = f32[16,24576]{1,0:T(8,128)} reduce(f32[16,1,24576]{2,1,0:T(1,128)S(1)} %all_to_all.41, f32[]{:T(128)} %broadcast.49), dimensions={1}, to_apply=%all_to_all.34.reduce_sub_computation | reduce | bytes 3145732 | tf_op jit(solution)/shard_map/all_to_all | solution.py:109
  306.7 3.4 reshape.128
  310.1 3.8 copy.71
  313.9 4.0 fusion.12
  317.9 0.0 all-reduce.3.cloned.1.call-update
  318.6 175.0 %all-reduce.3.cloned.1.call-done = f32[16,2,64,192]{3,0,2,1:T(8,128)} async-done(((f32[16,2,64,192]{3,0,2,1:T(8,128)}), f32[16,2,64,192]{3,0,2,1:T(8,128)}) %all-reduce.3.cloned.1.call-update) | async-done | bytes 1572880 | tf_op jit(solution)/shard_map/psum | solution.py:113
  493.6 1.3 dynamic-slice_bitcast_fusion
  494.9 0.6 copy.65
  495.5 0.6 copy.66
  (2 shorter events, 0.0 us)
Async XLA Ops:
  7.2 11.9 %copy-start = (bf16[1,192,3072]{2,1,0:T(8,128)(2,1)S(1)}, bf16[1,192,3072]{2,1,0:T(8,128)(2,1)}, u32[]{:S(2)}) copy-start(bf16[1,192,3072]{2,1,0:T(8,128)(2,1)} %param.11) | copy-start | bytes 3538948
  7.2 221.4 %all-gather.2.cloned.1.call-start = ((), (), s32[]{:S(2)}) async-start(), calls=%async_computation.3 | async-start | bytes 20054016 | tf_op jit(solution)/shard_map/all_gather | solution.py:55
  9.8 61.7 %all-to-all-start = ((bf16[16,1,2,64,192]{4,3,2,1,0:T(8,128)(2,1)}), bf16[16,1,2,64,192]{4,3,2,1,0:T(8,128)(2,1)S(1)}, u32[]{:S(2)}, u32[]{:S(2)}) async-start(bf16[16,1,2,64,192]{4,3,2,1,0:T(8,128)(2,1)} %stack.20), calls=%async_computation | async-start | bytes 2097152 | tf_op jit(solution)/shard_map/all_to_all | solution.py:65
  18.3 1.3 copy-start.1
  19.0 1.4 copy-start.2
  19.6 2.8 copy-start.7
  19.6 31.3 %copy-start.6 = (s32[16]{0:T(128)S(1)}, s32[16]{0:T(128)}, u32[]{:S(2)}) copy-start(s32[16]{0:T(128)} %param.20) | copy-start | bytes 196
  73.6 94.3 %all-to-all-start.1 = ((bf16[16,2,64,192]{3,2,1,0:T(8,128)(2,1)}), bf16[16,2,64,192]{3,2,1,0:T(8,128)(2,1)S(1)}, u32[]{:S(2)}, u32[]{:S(2)}) async-start(bf16[16,2,64,192]{3,2,1,0:T(8,128)(2,1)} %copy.61), calls=%async_computation.1 | async-start | bytes 2097152 | tf_op jit(solution)/shard_map/all_to_all | solution.py:73
  82.3 411.3 %all-reduce.3.cloned.1.call-start = ((), (), s32[]{:S(2)}) async-start(), calls=%async_computation.4 | async-start | bytes 4194304 | tf_op jit(solution)/shard_map/psum | solution.py:113
  83.2 2.0 copy-start.3
  87.1 141.5 %copy-start.4 = (bf16[1,192,24,128]{3,2,1,0:T(8,128)(2,1)}, bf16[1,192,24,128]{3,2,1,0:T(8,128)(2,1)S(1)}, u32[]{:S(2)}) copy-start(bf16[1,192,24,128]{3,2,1,0:T(8,128)(2,1)S(1)} %copy.58) | copy-start | bytes 3538948
  228.6 9.1 %copy-start.5 = (bf16[1,192,3072]{2,1,0:T(8,128)(2,1)S(1)}, bf16[1,192,3072]{2,1,0:T(8,128)(2,1)}, u32[]{:S(2)}) copy-start(bf16[1,192,3072]{2,1,0:T(8,128)(2,1)} %param.15) | copy-start | bytes 3538948
Sparse Core Ops, SparseCore 0:
  10.7 217.8 all-gather.1
  318.1 175.5 all-reduce.2
